TPU v7x, 32 devices: a whole 2x2x4 slice. The times are simulated.
32 devices in a mesh: gx: 2 (over x), gy: 4 (over y, core), gz: 4 (over z).
Axes of the slice: x: 2, y: 2, z: 4, core: 2. Of those that a mesh axis runs over, the one named last changes fastest.
Arguments:
- right_side: float32 [32, 64, 1024], P('gx', 'gy', 'gz'), may hold values from -5 to 5
- coefficients: float32 [4, 32, 64, 1024], P(None, 'gx', 'gy', 'gz'), may hold values from 0.1 to 32
- first_guess: float32 [32, 64, 1024], P('gx', 'gy', 'gz'), may hold values from -3 to 3
Outputs:
- solution_field: float32 [32, 64, 1024], P('gx', 'gy', 'gz')
All inputs are finite; a program needn't handle non-finite values.
Results may differ from a plain program's by a relative error of at most 0.00002.
Values sent between devices are 32-bit elements; how exact they have to be, the bound alone decides.
A program may use at most 128 MiB of HBM per device.

v0:
```python
import jax
import jax.numpy as jnp
from jax import lax
from jax.sharding import PartitionSpec as P

CYCLES = 2
SWEEPS = 8


relaxation = 0.8
blending = 0.4


def with_halo(block, sides, width):
    for axis, dim in sides:
        count = lax.axis_size(axis)
        forward = [(i, i + 1) for i in range(count - 1)]
        backward = [(target, source) for source, target in forward]
        low = lax.ppermute(
            lax.slice_in_dim(block, block.shape[dim] - width, None, axis=dim), axis, forward
        )
        high = lax.ppermute(lax.slice_in_dim(block, 0, width, axis=dim), axis, backward)
        block = jnp.concatenate([low, block, high], axis=dim)
    return block


def shifted(values, direction, start):
    starts = [1, 1, 1]
    starts[direction] = start
    limits = [
        starts[0] + values.shape[0] - 2,
        starts[1] + values.shape[1] - 2,
        starts[2] + values.shape[2] - 2,
    ]
    return lax.slice(values, starts, limits)


def trimmed(values, depth):
    if depth == 0:
        return values
    return values[depth:-depth, depth:-depth, depth:-depth]


def trimmed_weights(weights, depth):
    return [
        (trimmed(weight_high, depth), trimmed(weight_low, depth))
        for weight_high, weight_low in weights
    ]


def region_weights(widened):
    reaction = shifted(widened[3], 0, 1)
    diagonal = reaction
    weights = []
    for direction in range(3):
        centre = shifted(widened[direction], 0, 1)
        weight_high = 0.5 * (centre + shifted(widened[direction], direction, 2))
        weight_low = 0.5 * (centre + shifted(widened[direction], direction, 0))
        weights.append((weight_high, weight_low))
        diagonal = diagonal + weight_high + weight_low
    return (reaction, weights, diagonal)


def stencil(padded, reaction, weights):
    middle = shifted(padded, 0, 1)
    result = reaction * middle
    for direction in range(3):
        weight_high, weight_low = weights[direction]
        upper_cells = shifted(padded, direction, 2)
        lower_cells = shifted(padded, direction, 0)
        result = result + (
            weight_high * (middle - upper_cells) + weight_low * (middle - lower_cells)
        )
    return result


def pair_mean(values, direction):
    shape = values.shape
    split_shape = shape[:direction] + (shape[direction] // 2, 2) + shape[direction + 1 :]
    paired = values.reshape(split_shape)
    even_cells = lax.index_in_dim(paired, 0, direction + 1, keepdims=False)
    odd_cells = lax.index_in_dim(paired, 1, direction + 1, keepdims=False)
    return 0.5 * (even_cells + odd_cells)


def coarse_fields(fields, direction):
    averaged = pair_mean(fields, direction + 1)
    factors = [1.0, 1.0, 1.0, 1.0]
    factors[direction] = 0.25
    return jnp.stack([averaged[member] * factors[member] for member in range(4)])


def prolong_padded(padded, direction):
    length = padded.shape[direction] - 2
    middle = lax.slice_in_dim(padded, 1, length + 1, axis=direction)
    upper_cells = lax.slice_in_dim(padded, 2, length + 2, axis=direction)
    lower_cells = lax.slice_in_dim(padded, 0, length, axis=direction)
    even_cells = 0.75 * middle + 0.25 * lower_cells
    odd_cells = 0.75 * middle + 0.25 * upper_cells
    joined = jnp.stack([even_cells, odd_cells], direction + 1)
    new_shape = list(middle.shape)
    new_shape[direction] = 2 * length
    return joined.reshape(new_shape)


def keep_along(values, direction):
    starts = [1, 1, 1]
    starts[direction] = 0
    limits = [values.shape[0] - 1, values.shape[1] - 1, values.shape[2] - 1]
    limits[direction] = values.shape[direction]
    return lax.slice(values, starts, limits)


def refresh_errors(errors):
    return with_halo(errors, (("gx", 0), ("gy", 1), ("gz", 2)), 4)


def deep_sweeps(coarse_residual, reaction, weights, diagonal, inside):
    widened_residual = with_halo(coarse_residual, (("gx", 0), ("gy", 1), ("gz", 2)), 4)
    errors = inside * (relaxation * widened_residual / diagonal)
    depth = 4
    for repeat in range(SWEEPS - 1):
        if depth == 0:
            errors = refresh_errors(errors)
            depth = 4
        level = depth - 1
        cut = 4 - level
        step_term = (
            relaxation
            * (
                trimmed(widened_residual, cut)
                - stencil(errors, trimmed(reaction, cut), trimmed_weights(weights, cut))
            )
            / trimmed(diagonal, cut)
        )
        errors = trimmed(errors, 1) + trimmed(inside, cut) * step_term
        depth = level
    return trimmed(errors, depth - 1)


def body(right_side, coefficients, first_guess):
    widened = with_halo(coefficients, (("gx", 1), ("gy", 2), ("gz", 3)), 1)
    reaction, weights, diagonal = region_weights(widened)
    branches = []
    for direction in range(3):
        coarse = coarse_fields(coefficients, direction)
        ones_field = jnp.ones_like(coarse[0])
        stacked = jnp.concatenate([coarse, ones_field[None]], 0)
        widened_coarse = with_halo(stacked, (("gx", 1), ("gy", 2), ("gz", 3)), 5)
        coarse_reaction, coarse_weights, coarse_diagonal = region_weights(widened_coarse[:4])
        inside = shifted(widened_coarse[4], 0, 1)
        coarse_diagonal = jnp.where(inside > 0.5, coarse_diagonal, 1.0)
        branches.append((coarse_reaction, coarse_weights, coarse_diagonal, inside))
    solution_field = first_guess
    for cycle_index in range(CYCLES):
        padded = with_halo(solution_field, (("gx", 0), ("gy", 1), ("gz", 2)), 1)
        residual = right_side - stencil(padded, reaction, weights)
        update = None
        for direction in range(3):
            coarse_reaction, coarse_weights, coarse_diagonal, inside = branches[direction]
            coarse_residual = pair_mean(residual, direction)
            rimmed = deep_sweeps(
                coarse_residual, coarse_reaction, coarse_weights, coarse_diagonal, inside
            )
            correction = prolong_padded(keep_along(rimmed, direction), direction)
            update = correction if update is None else update + correction
        solution_field = solution_field + blending * update
    return solution_field


def solution(mesh):
    in_specs = (P("gx", "gy", "gz"), P(None, "gx", "gy", "gz"), P("gx", "gy", "gz"))
    out_specs = P("gx", "gy", "gz")
    return jax.shard_map(body, mesh=mesh, in_specs=in_specs, out_specs=out_specs, check_vma=False)
```

profile of v0, /device:TPU:0, one launch (start us, length us, event | category | flops | bytes accessed | tf_op | source)
XLA Modules:
  0.0 614.3 jit_solution(13042484588289120510)
XLA Ops:
  0.0 7.1 %copy.770 = f32[4,16,16,256]{2,1,3,0:T(8,128)} copy(f32[4,16,16,256]{3,2,1,0:T(8,128)} %param.4) | data formatting | bytes 2097152 | tf_op args[1]
  19.7 6.2 %collective-permute-start.48 = (f32[5,5,16,128]{3,2,1,0:T(8,128)}, f32[5,5,16,128]{3,2,1,0:T(8,128)}, u32[]{:S(2)}, u32[]{:S(2)}) collective-permute-start(f32[5,5,16,128]{3,2,1,0:T(8,128)} %get-tuple-element.85), channel_id=1, source_target_pairs={{0,16},{1,17},{2,18},{3,19},{4,20},{5,21},{6,22},{7,23},{8,24},{9,... | collective-permute-start | bytes 614408 | tf_op jit(solution)/shard_map/ppermute | solution.py:19
  29.3 4.5 collective-permute-start.6
  46.8 5.9 collective-permute-start.8
  90.2 4.5 collective-permute-start.54
  116.9 4.7 collective-permute-start.18
  130.0 5.9 collective-permute-start.20
  143.4 6.4 %collective-permute-start.38 = (f32[24,4,256]{2,0,1:T(8,128)}, f32[24,4,256]{2,0,1:T(8,128)S(1)}, u32[]{:S(2)}, u32[]{:S(2)}) collective-permute-start(f32[24,4,256]{2,0,1:T(8,128)} %get-tuple-element.155), channel_id=1, source_target_pairs={{0,4},{4,8},{8,12},{1,5},{5,9},{9,13},{2,6},{6,10},{10,14},{3,7},{... | collective-permute-start | bytes 294920 | tf_op jit(solution)/shard_map/ppermute | solution.py:19
  163.8 5.8 collective-permute-start.52
  171.3 5.6 collective-permute-done.53
  180.9 5.7 collective-permute-start.58
  189.9 7.0 %pad_maximum_fusion.2 = f32[5,26,26,138]{3,2,1,0:T(8,128)S(1)} fusion(f32[5,26,26,5]{3,2,1,0:T(8,128)S(1)} %copy.781, f32[5,26,5,128]{3,2,1,0:T(8,128)S(1)} %copy.777, f32[5,5,16,128]{3,2,1,0:T(8,128)} %collective-permute-done.49, f32[1,16,16,128]{3,2,1,0:T(8,128)} %copy-done.123, f32[1,16,16,128]{3,2,1,0:T(8,128)S(1)} %copy-done.121, ...), kind=kLoop, calls=%fused_computation.2 | loop fusion | flops 4197960 | bytes 3731520 | tf_op jit(solution)/shard_map/concatenate | solution.py:23
  209.4 4.5 collective-permute-start.60
  227.1 4.9 collective-permute-start.64
  237.6 5.2 collective-permute-start.2
  257.7 5.0 collective-permute-start.22
  277.9 6.1 collective-permute-start.4
  305.0 7.4 %pad_maximum_fusion = f32[5,18,26,266]{3,2,1,0:T(8,128)S(1)} fusion(f32[5,18,26,5]{3,2,1,0:T(8,128)} %copy.750, f32[5,18,5,256]{3,2,1,0:T(8,128)} %copy-done.91, f32[5,5,16,256]{3,2,1,0:T(8,128)} %collective-permute-done.1, f32[1,8,16,256]{3,2,1,0:T(8,128)} %copy-done.110, f32[3,8,16,256]{3,2,1,0:T(8,128)} %copy-done.78, f32[1,8,16,256]{3,2,1,0:T(8,128)} %copy-done.107, ...), kind=kLoop, calls=%fused_computation | loop fusion | flops 4979520 | bytes 4979520 | tf_op jit(solution)/shard_map/concatenate | solution.py:23
  312.8 5.3 collective-permute-start.34
  334.5 8.8 %pad_maximum_fusion.1 = f32[5,26,18,266]{3,1,2,0:T(8,128)S(1)} fusion(f32[5,26,18,5]{3,1,2,0:T(8,128)} %copy.764, f32[5,26,5,256]{3,1,2,0:T(8,128)} %collective-permute-done.33, f32[5,5,8,256]{3,1,2,0:T(8,128)} %copy-done.125, f32[1,16,8,256]{3,1,2,0:T(8,128)} %copy-done.105, f32[2,16,8,256]{3,1,2,0:T(8,128)S(1)} %copy-done.94, ...), kind=kLoop, calls=%fused_computation.1 | loop fusion | flops 5601960 | bytes 4979520 | tf_op jit(solution)/shard_map/concatenate | solution.py:23
  355.7 4.5 collective-permute-start.42
  361.7 4.5 collective-permute-start.24
  379.5 4.6 collective-permute-start.28
  385.6 4.7 collective-permute-start.46
  446.2 4.5 collective-permute-start.96
  452.9 4.5 collective-permute-start.72
  471.3 4.6 collective-permute-start.100
  509.5 4.6 collective-permute-start.76
  544.5 4.5 collective-permute-start.78
  550.7 4.6 collective-permute-start.106
  583.7 4.6 collective-permute-start.82
  590.7 4.7 collective-permute-start.94
  (810 shorter events, 437.4 us)
Async XLA Ops:
  18.4 98.4 %collective-permute-start.49 = (f32[5,5,16,128]{3,2,1,0:T(8,128)}, f32[5,5,16,128]{3,2,1,0:T(8,128)}, u32[]{:S(2)}, u32[]{:S(2)}) collective-permute-start(f32[5,5,16,128]{3,2,1,0:T(8,128)} %get-tuple-element.86), channel_id=1, source_target_pairs={{16,0},{17,1},{18,2},{19,3},{20,4},{21,5},{22,6},{23,7},{24,8},{25... | collective-permute-start | bytes 614408 | tf_op jit(solution)/shard_map/ppermute | solution.py:22
  19.7 101.8 %collective-permute-start.48 = (f32[5,5,16,128]{3,2,1,0:T(8,128)}, f32[5,5,16,128]{3,2,1,0:T(8,128)}, u32[]{:S(2)}, u32[]{:S(2)}) collective-permute-start(f32[5,5,16,128]{3,2,1,0:T(8,128)} %get-tuple-element.85), channel_id=1, source_target_pairs={{0,16},{1,17},{2,18},{3,19},{4,20},{5,21},{6,22},{7,23},{8,24},{9,... | collective-permute-start | bytes 614408 | tf_op jit(solution)/shard_map/ppermute | solution.py:19
  38.6 179.8 %collective-permute-start.1 = (f32[5,5,16,256]{3,2,1,0:T(8,128)}, f32[5,5,16,256]{3,2,1,0:T(8,128)}, u32[]{:S(2)}, u32[]{:S(2)}) collective-permute-start(f32[5,5,16,256]{3,2,1,0:T(8,128)} %get-tuple-element.84), channel_id=1, source_target_pairs={{16,0},{17,1},{18,2},{19,3},{20,4},{21,5},{22,6},{23,7},{24,8},{25... | collective-permute-start | bytes 1228808 | tf_op jit(solution)/shard_map/ppermute | solution.py:22
  111.4 108.3 %collective-permute-start = (f32[5,5,16,256]{3,2,1,0:T(8,128)}, f32[5,5,16,256]{3,2,1,0:T(8,128)}, u32[]{:S(2)}, u32[]{:S(2)}) collective-permute-start(f32[5,5,16,256]{3,2,1,0:T(8,128)} %get-tuple-element.83), channel_id=1, source_target_pairs={{0,16},{1,17},{2,18},{3,19},{4,20},{5,21},{6,22},{7,23},{8,24},{9,... | collective-permute-start | bytes 1228808 | tf_op jit(solution)/shard_map/ppermute | solution.py:19
  127.3 35.1 %collective-permute-start.39 = (f32[24,4,256]{2,0,1:T(8,128)}, f32[24,4,256]{2,0,1:T(8,128)}, u32[]{:S(2)}, u32[]{:S(2)}) collective-permute-start(f32[24,4,256]{2,0,1:T(8,128)} %get-tuple-element.156), channel_id=1, source_target_pairs={{4,0},{8,4},{12,8},{5,1},{9,5},{13,9},{6,2},{10,6},{14,10},{7,3},{... | collective-permute-start | bytes 294920 | tf_op jit(solution)/shard_map/ppermute | solution.py:22
  143.4 20.3 %collective-permute-start.38 = (f32[24,4,256]{2,0,1:T(8,128)}, f32[24,4,256]{2,0,1:T(8,128)S(1)}, u32[]{:S(2)}, u32[]{:S(2)}) collective-permute-start(f32[24,4,256]{2,0,1:T(8,128)} %get-tuple-element.155), channel_id=1, source_target_pairs={{0,4},{4,8},{8,12},{1,5},{5,9},{9,13},{2,6},{6,10},{10,14},{3,7},{... | collective-permute-start | bytes 294920 | tf_op jit(solution)/shard_map/ppermute | solution.py:19
  150.1 126.5 %collective-permute-start.33 = (f32[5,26,5,256]{3,1,2,0:T(8,128)}, f32[5,26,5,256]{3,1,2,0:T(8,128)}, u32[]{:S(2)}, u32[]{:S(2)}) collective-permute-start(f32[5,26,5,256]{3,1,2,0:T(8,128)} %get-tuple-element.74), channel_id=1, source_target_pairs={{4,0},{8,4},{12,8},{5,1},{9,5},{13,9},{6,2},{10,6},{14,10},{7,3},{... | collective-permute-start | bytes 1996808 | tf_op jit(solution)/shard_map/ppermute | solution.py:22
  163.8 17.2 %collective-permute-start.52 = (f32[5,26,26,5]{2,1,3,0:T(8,128)}, f32[5,26,26,5]{2,1,3,0:T(8,128)}, u32[]{:S(2)}, u32[]{:S(2)}) collective-permute-start(f32[5,26,26,5]{2,1,3,0:T(8,128)} %copy.778), channel_id=1, source_target_pairs={{0,1},{1,2},{2,3},{4,5},{5,6},{6,7},{8,9},{9,10},{10,11},{12,13},{... | collective-permute-start | bytes 202808 | tf_op jit(solution)/shard_map/ppermute | solution.py:19
  177.7 19.6 %collective-permute-start.59 = (f32[24,24,4]{2,1,0:T(8,128)}, f32[24,24,4]{2,1,0:T(8,128)}, u32[]{:S(2)}, u32[]{:S(2)}) collective-permute-start(f32[24,24,4]{2,1,0:T(8,128)} %get-tuple-element.130), channel_id=1, source_target_pairs={{1,0},{2,1},{3,2},{5,4},{6,5},{7,6},{9,8},{10,9},{11,10},{13,12},{... | collective-permute-start | bytes 27656 | tf_op jit(solution)/shard_map/ppermute | solution.py:22
  180.9 16.4 %collective-permute-start.58 = (f32[24,24,4]{2,1,0:T(8,128)}, f32[24,24,4]{2,1,0:T(8,128)}, u32[]{:S(2)}, u32[]{:S(2)}) collective-permute-start(f32[24,24,4]{2,1,0:T(8,128)} %get-tuple-element.129), channel_id=1, source_target_pairs={{0,1},{1,2},{2,3},{4,5},{5,6},{6,7},{8,9},{9,10},{10,11},{12,13},{... | collective-permute-start | bytes 27656 | tf_op jit(solution)/shard_map/ppermute | solution.py:19
  214.7 63.2 %collective-permute-start.32 = (f32[5,26,5,256]{3,1,2,0:T(8,128)}, f32[5,26,5,256]{3,1,2,0:T(8,128)}, u32[]{:S(2)}, u32[]{:S(2)}) collective-permute-start(f32[5,26,5,256]{3,1,2,0:T(8,128)} %get-tuple-element.73), channel_id=1, source_target_pairs={{0,4},{4,8},{8,12},{1,5},{5,9},{9,13},{2,6},{6,10},{10,14},{3,7},{... | collective-permute-start | bytes 1996808 | tf_op jit(solution)/shard_map/ppermute | solution.py:19
  217.1 95.7 %collective-permute-start.23 = (f32[16,24,4]{2,1,0:T(8,128)}, f32[16,24,4]{2,1,0:T(8,128)}, u32[]{:S(2)}, u32[]{:S(2)}) collective-permute-start(f32[16,24,4]{2,1,0:T(8,128)} %get-tuple-element.112), channel_id=1, source_target_pairs={{1,0},{2,1},{3,2},{5,4},{6,5},{7,6},{9,8},{10,9},{11,10},{13,12},{... | collective-permute-start | bytes 18440 | tf_op jit(solution)/shard_map/ppermute | solution.py:22
  235.8 21.8 %collective-permute-start.3 = (f32[5,18,5,256]{3,1,2,0:T(8,128)}, f32[5,18,5,256]{3,1,2,0:T(8,128)}, u32[]{:S(2)}, u32[]{:S(2)}) collective-permute-start(f32[5,18,5,256]{3,1,2,0:T(8,128)} %copy.744), channel_id=1, source_target_pairs={{4,0},{8,4},{12,8},{5,1},{9,5},{13,9},{6,2},{10,6},{14,10},{7,3},{... | collective-permute-start | bytes 1382408 | tf_op jit(solution)/shard_map/ppermute | solution.py:22
  237.6 26.4 %collective-permute-start.2 = (f32[5,18,5,256]{3,1,2,0:T(8,128)}, f32[5,18,5,256]{3,1,2,0:T(8,128)}, u32[]{:S(2)}, u32[]{:S(2)}) collective-permute-start(f32[5,18,5,256]{3,1,2,0:T(8,128)} %copy.743), channel_id=1, source_target_pairs={{0,4},{4,8},{8,12},{1,5},{5,9},{9,13},{2,6},{6,10},{10,14},{3,7},{... | collective-permute-start | bytes 1382408 | tf_op jit(solution)/shard_map/ppermute | solution.py:19
  257.7 60.4 %collective-permute-start.22 = (f32[16,24,4]{2,1,0:T(8,128)}, f32[16,24,4]{2,1,0:T(8,128)}, u32[]{:S(2)}, u32[]{:S(2)}) collective-permute-start(f32[16,24,4]{2,1,0:T(8,128)} %get-tuple-element.111), channel_id=1, source_target_pairs={{0,1},{1,2},{2,3},{4,5},{5,6},{6,7},{8,9},{9,10},{10,11},{12,13},{... | collective-permute-start | bytes 18440 | tf_op jit(solution)/shard_map/ppermute | solution.py:19
  264.0 79.7 %collective-permute-start.41 = (f32[24,16,4]{2,0,1:T(8,128)}, f32[24,16,4]{2,0,1:T(8,128)}, u32[]{:S(2)}, u32[]{:S(2)}) collective-permute-start(f32[24,16,4]{2,0,1:T(8,128)} %get-tuple-element.108), channel_id=1, source_target_pairs={{1,0},{2,1},{3,2},{5,4},{6,5},{7,6},{9,8},{10,9},{11,10},{13,12},{... | collective-permute-start | bytes 18440 | tf_op jit(solution)/shard_map/ppermute | solution.py:22
  276.6 17.5 %collective-permute-start.5 = (f32[5,18,26,5]{2,1,3,0:T(8,128)}, f32[5,18,26,5]{2,1,3,0:T(8,128)}, u32[]{:S(2)}, u32[]{:S(2)}) collective-permute-start(f32[5,18,26,5]{2,1,3,0:T(8,128)} %copy.748), channel_id=1, source_target_pairs={{1,0},{2,1},{3,2},{5,4},{6,5},{7,6},{9,8},{10,9},{11,10},{13,12},{... | collective-permute-start | bytes 140408 | tf_op jit(solution)/shard_map/ppermute | solution.py:22
  277.9 22.9 %collective-permute-start.4 = (f32[5,18,26,5]{2,1,3,0:T(8,128)}, f32[5,18,26,5]{2,1,3,0:T(8,128)}, u32[]{:S(2)}, u32[]{:S(2)}) collective-permute-start(f32[5,18,26,5]{2,1,3,0:T(8,128)} %copy.747), channel_id=1, source_target_pairs={{0,1},{1,2},{2,3},{4,5},{5,6},{6,7},{8,9},{9,10},{10,11},{12,13},{... | collective-permute-start | bytes 140408 | tf_op jit(solution)/shard_map/ppermute | solution.py:19
  294.2 49.5 %collective-permute-start.40 = (f32[24,16,4]{2,0,1:T(8,128)}, f32[24,16,4]{2,0,1:T(8,128)}, u32[]{:S(2)}, u32[]{:S(2)}) collective-permute-start(f32[24,16,4]{2,0,1:T(8,128)} %get-tuple-element.107), channel_id=1, source_target_pairs={{0,1},{1,2},{2,3},{4,5},{5,6},{6,7},{8,9},{9,10},{10,11},{12,13},{... | collective-permute-start | bytes 18440 | tf_op jit(solution)/shard_map/ppermute | solution.py:19
  300.9 27.9 %collective-permute-start.35 = (f32[5,26,18,5]{1,2,3,0:T(8,128)}, f32[5,26,18,5]{1,2,3,0:T(8,128)}, u32[]{:S(2)}, u32[]{:S(2)}) collective-permute-start(f32[5,26,18,5]{1,2,3,0:T(8,128)} %copy.762), channel_id=1, source_target_pairs={{1,0},{2,1},{3,2},{5,4},{6,5},{7,6},{9,8},{10,9},{11,10},{13,12},{... | collective-permute-start | bytes 140408 | tf_op jit(solution)/shard_map/ppermute | solution.py:22
  312.8 18.8 %collective-permute-start.34 = (f32[5,26,18,5]{1,2,3,0:T(8,128)}, f32[5,26,18,5]{1,2,3,0:T(8,128)}, u32[]{:S(2)}, u32[]{:S(2)}) collective-permute-start(f32[5,26,18,5]{1,2,3,0:T(8,128)} %copy.761), channel_id=1, source_target_pairs={{0,1},{1,2},{2,3},{4,5},{5,6},{6,7},{8,9},{9,10},{10,11},{12,13},{... | collective-permute-start | bytes 140408 | tf_op jit(solution)/shard_map/ppermute | solution.py:19
  446.2 18.1 %collective-permute-start.96 = (f32[4,16,128]{2,1,0:T(8,128)S(1)}, f32[4,16,128]{2,1,0:T(8,128)S(1)}, u32[]{:S(2)}, u32[]{:S(2)}) collective-permute-start(f32[4,16,128]{2,1,0:T(8,128)S(1)} %get-tuple-element.171), channel_id=1, source_target_pairs={{0,16},{1,17},{2,18},{3,19},{4,20},{5,21},{6,22},{7,23},{8,24},{9,... | collective-permute-start | bytes 98312 | tf_op jit(solution)/shard_map/ppermute | solution.py:19
  451.6 41.9 %collective-permute-start.73 = (f32[4,16,256]{2,1,0:T(8,128)S(1)}, f32[4,16,256]{2,1,0:T(8,128)S(1)}, u32[]{:S(2)}, u32[]{:S(2)}) collective-permute-start(f32[4,16,256]{2,1,0:T(8,128)S(1)} %get-tuple-element.168), channel_id=1, source_target_pairs={{16,0},{17,1},{18,2},{19,3},{20,4},{21,5},{22,6},{23,7},{24,8},{25... | collective-permute-start | bytes 196616 | tf_op jit(solution)/shard_map/ppermute | solution.py:22
  452.9 45.2 %collective-permute-start.72 = (f32[4,16,256]{2,1,0:T(8,128)S(1)}, f32[4,16,256]{2,1,0:T(8,128)S(1)}, u32[]{:S(2)}, u32[]{:S(2)}) collective-permute-start(f32[4,16,256]{2,1,0:T(8,128)S(1)} %get-tuple-element.167), channel_id=1, source_target_pairs={{0,16},{1,17},{2,18},{3,19},{4,20},{5,21},{6,22},{7,23},{8,24},{9,... | collective-permute-start | bytes 196616 | tf_op jit(solution)/shard_map/ppermute | solution.py:19
  475.9 33.6 %collective-permute-start.87 = (f32[24,4,256]{2,0,1:T(8,128)S(1)}, f32[24,4,256]{2,0,1:T(8,128)S(1)}, u32[]{:S(2)}, u32[]{:S(2)}) collective-permute-start(f32[24,4,256]{2,0,1:T(8,128)S(1)} %get-tuple-element.148), channel_id=1, source_target_pairs={{4,0},{8,4},{12,8},{5,1},{9,5},{13,9},{6,2},{10,6},{14,10},{7,3},{... | collective-permute-start | bytes 294920 | tf_op jit(solution)/shard_map/ppermute | solution.py:22
  481.7 32.4 %collective-permute-start.86 = (f32[24,4,256]{2,0,1:T(8,128)S(1)}, f32[24,4,256]{2,0,1:T(8,128)S(1)}, u32[]{:S(2)}, u32[]{:S(2)}) collective-permute-start(f32[24,4,256]{2,0,1:T(8,128)S(1)} %get-tuple-element.147), channel_id=1, source_target_pairs={{0,4},{4,8},{8,12},{1,5},{5,9},{9,13},{2,6},{6,10},{10,14},{3,7},{... | collective-permute-start | bytes 294920 | tf_op jit(solution)/shard_map/ppermute | solution.py:19
  502.5 46.6 %collective-permute-start.105 = (f32[24,4,128]{2,0,1:T(8,128)S(1)}, f32[24,4,128]{2,0,1:T(8,128)S(1)}, u32[]{:S(2)}, u32[]{:S(2)}) collective-permute-start(f32[24,4,128]{2,0,1:T(8,128)S(1)} %copy.813), channel_id=1, source_target_pairs={{4,0},{8,4},{12,8},{5,1},{9,5},{13,9},{6,2},{10,6},{14,10},{7,3},{... | collective-permute-start | bytes 147464 | tf_op jit(solution)/shard_map/ppermute | solution.py:22
  503.9 45.3 %collective-permute-start.104 = (f32[24,4,128]{2,0,1:T(8,128)S(1)}, f32[24,4,128]{2,0,1:T(8,128)S(1)}, u32[]{:S(2)}, u32[]{:S(2)}) collective-permute-start(f32[24,4,128]{2,0,1:T(8,128)S(1)} %copy.812), channel_id=1, source_target_pairs={{0,4},{4,8},{8,12},{1,5},{5,9},{9,13},{2,6},{6,10},{10,14},{3,7},{... | collective-permute-start | bytes 147464 | tf_op jit(solution)/shard_map/ppermute | solution.py:19
  543.2 25.8 %collective-permute-start.79 = (f32[4,16,256]{2,1,0:T(8,128)S(1)}, f32[4,16,256]{2,1,0:T(8,128)S(1)}, u32[]{:S(2)}, u32[]{:S(2)}) collective-permute-start(f32[4,16,256]{2,1,0:T(8,128)S(1)} %get-tuple-element.166), channel_id=1, source_target_pairs={{16,0},{17,1},{18,2},{19,3},{20,4},{21,5},{22,6},{23,7},{24,8},{25... | collective-permute-start | bytes 196616 | tf_op jit(solution)/shard_map/ppermute | solution.py:22
  544.5 24.5 %collective-permute-start.78 = (f32[4,16,256]{2,1,0:T(8,128)S(1)}, f32[4,16,256]{2,1,0:T(8,128)S(1)}, u32[]{:S(2)}, u32[]{:S(2)}) collective-permute-start(f32[4,16,256]{2,1,0:T(8,128)S(1)} %get-tuple-element.165), channel_id=1, source_target_pairs={{0,16},{1,17},{2,18},{3,19},{4,20},{5,21},{6,22},{7,23},{8,24},{9,... | collective-permute-start | bytes 196616 | tf_op jit(solution)/shard_map/ppermute | solution.py:19
  556.0 32.3 %collective-permute-start.93 = (f32[24,4,256]{2,0,1:T(8,128)}, f32[24,4,256]{2,0,1:T(8,128)}, u32[]{:S(2)}, u32[]{:S(2)}) collective-permute-start(f32[24,4,256]{2,0,1:T(8,128)} %get-tuple-element.146), channel_id=1, source_target_pairs={{4,0},{8,4},{12,8},{5,1},{9,5},{13,9},{6,2},{10,6},{14,10},{7,3},{... | collective-permute-start | bytes 294920 | tf_op jit(solution)/shard_map/ppermute | solution.py:22
  559.7 28.6 %collective-permute-start.92 = (f32[24,4,256]{2,0,1:T(8,128)}, f32[24,4,256]{2,0,1:T(8,128)}, u32[]{:S(2)}, u32[]{:S(2)}) collective-permute-start(f32[24,4,256]{2,0,1:T(8,128)} %get-tuple-element.145), channel_id=1, source_target_pairs={{0,4},{4,8},{8,12},{1,5},{5,9},{9,13},{2,6},{6,10},{10,14},{3,7},{... | collective-permute-start | bytes 294920 | tf_op jit(solution)/shard_map/ppermute | solution.py:19
  (263 other events, 3419.2 us)
where the time goes:
time: 624 us; the launch traced here: 614 us
  starting transfers between devices  300 us (48%)
  other arithmetic  159 us (25%)
  local copies, waits for them, and re-layouts  111 us (18%)
  waiting for transfers between devices  39.8 us (6%)
    ppermute x54, starting transfers between devices, with_halo(): lax.ppermute(lax.slice_in_dim(block, block.shape[dim] - width, None, axis...  228 us
    add x42, other arithmetic, deep_sweeps(): errors = trimmed(errors, 1) + trimmed(inside, cut) * step_term  83.9 us
    ppermute x54, starting transfers between devices, with_halo(): lax.ppermute(lax.slice_in_dim(block, 0, width, axis=dim), axis, backward)  71.3 us
    concatenate x36, other arithmetic, with_halo(): block = jnp.concatenate([low, block, high], axis=dim)  44.6 us
    ppermute x54, waiting for transfers between devices, with_halo(): lax.ppermute(lax.slice_in_dim(block, 0, width, axis=dim), axis, backward)  29.9 us
    slice x49, local copies, waits for them, and re-layouts, with_halo(): lax.slice_in_dim(block, block.shape[dim] - width, None, axis=dim)  28.3 us
    unnamed x386, local copies, waits for them, and re-layouts  20.3 us
    slice x13, local copies, waits for them, and re-layouts, with_halo(): lax.slice_in_dim(block, 0, width, axis=dim)  14.2 us
  transfers between devices with their start and end apart: 108, of which 19 were waited for; matrix products, arithmetic and copies ran while one was open for 33% of the time, Pallas kernels for 0%

commit v1 on v0

v1 whole, which is shorter than its diff:
```python
import functools

import jax
import jax.numpy as jnp
from jax import lax
from jax.experimental import pallas as pl
from jax.experimental.pallas import tpu as pltpu
from jax.sharding import PartitionSpec as P

CYCLES = 2
SWEEPS = 8
REACH = 2 * (SWEEPS + 1)
STEP = 20
LANES = 128
CHUNK = 2

relaxation = 0.8
blending = 0.4
MESH = pl.DeviceIdType.MESH
HIGH = lax.Precision.HIGHEST


def iota(shape, dim):
    return lax.broadcasted_iota(jnp.int32, shape, dim)


def matmul(a, b):
    return lax.dot_general(
        a, b, (((1,), (0,)), ((), ())), precision=HIGH, preferred_element_type=jnp.float32
    )


def kernel(sizes, names, b_ref, k_ref, g_ref, out_ref, *scratch):
    (fields, weights, diag, es, yss, yrs, ms, fs, kxr, kys, kyr, zs, zr, us, ur,
     send, recv, ksend, krecv, zsend, zrecv) = scratch
    nx, ny, nz = sizes
    wide = nz + LANES
    shapes = ((nx // 2, ny, wide), (nx, ny // 2, wide), (nx, ny, nz // 2 + LANES), (nx, ny, wide))
    place = [lax.axis_index(n) for n in names]
    counts = [lax.axis_size(n) for n in names]
    has_low = [p > 0 for p in place]
    has_high = [p < c - 1 for p, c in zip(place, counts)]
    ways = []
    for axis in range(3):
        ways.append((axis, -1, has_low[axis], has_high[axis]))
        ways.append((axis, 1, has_high[axis], has_low[axis]))

    def target(way):
        axis, step = ways[way][:2]
        return {names[axis]: place[axis] + step}

    def copy(src, dst, ssem, rsem, way):
        return pltpu.make_async_remote_copy(
            src_ref=src, dst_ref=dst, send_sem=ssem, recv_sem=rsem,
            device_id=target(way), device_id_type=MESH,
        )

    def start(copies):
        for way, c in copies:
            @pl.when(ways[way][2])
            def _():
                c.start()

    def finish(copies):
        for way, c in copies:
            @pl.when(ways[way][3])
            def _():
                c.wait_recv()
        for way, c in copies:
            @pl.when(ways[way][2])
            def _():
                c.wait_send()

    def faces(g, slot):
        x = shapes[g][0]
        e, ys, yr = es[g], yss[g], yrs[g]
        return [
            (0, copy(e.at[slot, 1], e.at[slot, x + 1], send.at[g, 0, slot], recv.at[g, 0, slot], 0)),
            (1, copy(e.at[slot, x], e.at[slot, 0], send.at[g, 1, slot], recv.at[g, 1, slot], 1)),
            (2, copy(ys.at[slot, 0], yr.at[slot, 1], send.at[g, 2, slot], recv.at[g, 2, slot], 2)),
            (3, copy(ys.at[slot, 1], yr.at[slot, 0], send.at[g, 3, slot], recv.at[g, 3, slot], 3)),
        ]

    for g in range(4):
        x = shapes[g][0]
        for slot in range(2):
            zero = jnp.zeros(shapes[g][1:], jnp.float32)
            es[g][slot, 0] = zero
            es[g][slot, x + 1] = zero
        yrs[g][...] = jnp.zeros(yrs[g].shape, jnp.float32)
    kxr[...] = jnp.zeros(kxr.shape, jnp.float32)
    kyr[...] = jnp.zeros(kyr.shape, jnp.float32)
    zr[...] = jnp.zeros(zr.shape, jnp.float32)
    ur[...] = jnp.zeros(ur.shape, jnp.float32)

    barrier = pltpu.get_barrier_semaphore()
    for way in range(6):
        @pl.when(ways[way][2])
        def _():
            pl.semaphore_signal(barrier, inc=1, device_id=target(way), device_id_type=MESH)
    peers = sum(jnp.where(has, 1, 0) for has in has_low + has_high)
    pl.semaphore_wait(barrier, peers)

    lane = iota((nx, ny, LANES), 2)
    low = jnp.zeros((nx, ny, LANES), jnp.float32)
    high = low
    for j in range(6):
        if j < 4:
            first, last = k_ref[j, :, :, :LANES], k_ref[j, :, :, nz - LANES:]
        elif j == 4:
            first, last = g_ref[:, :, :LANES], g_ref[:, :, nz - LANES:]
        else:
            first, last = b_ref[:, :, :LANES], b_ref[:, :, nz - LANES:]
        here = (lane >= STEP * j) & (lane < STEP * j + REACH)
        low = jnp.where(here, pltpu.roll(first, STEP * j, 2) if j else first, low)
        high = jnp.where(here, pltpu.roll(last, (STEP * j + REACH) % LANES, 2), high)
    zs[0] = low
    zs[1] = high
    deep = [
        (4, copy(zs.at[0], zr.at[1], zsend.at[0], zrecv.at[0], 4)),
        (5, copy(zs.at[1], zr.at[0], zsend.at[1], zrecv.at[1], 5)),
    ]
    start(deep)
    for j in range(4):
        fields[j, :, :, :nz] = k_ref[j]
    fields[4, :, :, :nz] = b_ref[...]
    es[3][0, 1:nx + 1, :, :nz] = g_ref[...]
    finish(deep)
    above, below = zr[1], zr[0]

    def beside(j):
        up = pltpu.roll(above, (LANES - STEP * j) % LANES, 2) if j else above
        down = pltpu.roll(below, (2 * LANES - REACH - STEP * j) % LANES, 2)
        return jnp.where(lane < REACH, up, jnp.where(lane >= LANES - REACH, down, 0.0))

    for j in range(4):
        fields[j, :, :, nz:] = beside(j)
    es[3][0, 1:nx + 1, :, nz:] = beside(4)
    fields[4, :, :, nz:] = beside(5)

    def send_guess(slot):
        u = es[3][slot, 1:nx + 1]
        yss[3][slot, 0] = u[:, 0:1, :]
        yss[3][slot, 1] = u[:, ny - 1:ny, :]
        start(faces(3, slot))

    ky = fields[1]
    for row in range(2):
        kys[0, row] = ky[:, row:row + 1, :]
        kys[1, row] = ky[:, ny - 2 + row:ny - 1 + row, :]
    edges = [
        (0, copy(fields.at[0, pl.ds(0, 2)], kxr.at[1], ksend.at[0], krecv.at[0], 0)),
        (1, copy(fields.at[0, pl.ds(nx - 2, 2)], kxr.at[0], ksend.at[1], krecv.at[1], 1)),
        (2, copy(kys.at[0], kyr.at[1], ksend.at[2], krecv.at[2], 2)),
        (3, copy(kys.at[1], kyr.at[0], ksend.at[3], krecv.at[3], 3)),
    ]
    start(edges)
    send_guess(0)

    half = nz // 2
    r, c = iota((wide, half + LANES), 0), iota((wide, half + LANES), 1)
    home = jnp.where(
        r < nz, r // 2,
        jnp.where(r < nz + LANES // 2, half + (r - nz) // 2, half + LANES // 2 + (r - nz) // 2),
    )
    z_mean = jnp.where(home == c, 0.5, 0.0).astype(jnp.float32)
    rows = nx * ny
    r, c = iota((rows // 2, rows), 0), iota((rows // 2, rows), 1)
    y_mean = jnp.where(c // 2 == r, 0.5, 0.0).astype(jnp.float32)
    r, c = iota((rows, rows), 0), iota((rows, rows), 1)
    weave = jnp.where(r // 2 + (r % 2) * (rows // 2) == c, 1.0, 0.0).astype(jnp.float32)
    r, c = iota((half + LANES, nz), 0), iota((half + LANES, nz), 1)
    main = c // 2
    total = half + LANES
    side = jnp.where(c % 2 == 1, main + 1, jnp.where(main == 0, total - 1, main - 1))
    z_spread = (jnp.where(r == main, 0.75, 0.0) + jnp.where(r == side, 0.25, 0.0)).astype(jnp.float32)

    def mean(values, d):
        if d == 0:
            paired = values.reshape((values.shape[0] // 2, 2) + values.shape[1:])
            return 0.5 * (paired[:, 0] + paired[:, 1])
        flat = values.reshape((values.shape[0] * ny, wide))
        if d == 1:
            return matmul(y_mean, flat).reshape((nx, ny // 2, wide))
        return matmul(flat, z_mean).reshape(shapes[2])

    def y_shift(values, halo_low, halo_high):
        y = values.shape[1]
        row = iota(values.shape, 1)
        lower = jnp.where(row == 0, halo_low, pltpu.roll(values, 1, 1))
        upper = jnp.where(row == y - 1, halo_high, pltpu.roll(values, y - 1, 1))
        return lower, upper

    def z_shift(values):
        return pltpu.roll(values, 1, 2), pltpu.roll(values, values.shape[2] - 1, 2)

    def face_weights(k0, k1, k2, s, x_low, x_high, y_low, y_high):
        pairs = [
            (jnp.concatenate([x_low, k0[:-1]], 0), jnp.concatenate([k0[1:], x_high], 0)),
            y_shift(k1, y_low, y_high),
            z_shift(k2),
        ]
        found = []
        total = s
        for k, pair in zip((k0, k1, k2), pairs):
            for other in pair:
                w = 0.5 * (k + other)
                found.append(w)
                total = total + w
        return found, total

    finish(edges)
    near_x = (kxr[0, 1:2], kxr[1, 0:1])
    near_y = (kyr[0, 1], kyr[1, 0])
    w, total_fine = face_weights(
        fields[0], fields[1], fields[2], fields[3], *near_x, *near_y)
    for j in range(6):
        weights[j] = w[j]
    diag[...] = total_fine

    for d in range(3):
        coarse = [mean(fields[j], d) for j in range(4)]
        coarse[d] = coarse[d] * 0.25
        if d == 0:
            x_faces = [0.125 * (kxr[side, 0:1] + kxr[side, 1:2]) for side in range(2)]
            y_faces = [
                0.5 * (v[:, 0] + v[:, 1])
                for v in [h.reshape((nx // 2, 2, 1, wide)) for h in near_y]
            ]
        elif d == 1:
            x_faces = [
                matmul(y_mean[: ny // 2, :ny], v[0])[None] for v in near_x
            ]
            y_faces = [0.125 * (kyr[side, 0] + kyr[side, 1]) for side in range(2)]
        else:
            x_faces = [matmul(v[0], z_mean)[None] for v in near_x]
            y_faces = [
                jnp.stack([matmul(jnp.broadcast_to(v[i], (8, wide)), z_mean)[0:1] for i in range(nx)])
                for v in near_y
            ]
        w, total_coarse = face_weights(*coarse, *x_faces, *y_faces)
        inside = coarse[3] > 0.0
        scale = jnp.where(inside, relaxation / jnp.where(inside, total_coarse, 1.0), 0.0)
        ms[d][6] = scale
        for j in range(6):
            ms[d][j] = w[j] * scale

    def sweep(g, slot, new_slot):
        e, yr, ys, m, f = es[g], yrs[g], yss[g], ms[g], fs[g]
        x, y, z = shapes[g]
        for x0 in range(0, x, CHUNK):
            planes = slice(x0, x0 + CHUNK)
            middle = e[slot, x0 + 1:x0 + 1 + CHUNK]
            y_low, y_high = y_shift(middle, yr[slot, 0, planes], yr[slot, 1, planes])
            z_low, z_high = z_shift(middle)
            new = (1.0 - relaxation) * middle + f[planes]
            new = new + m[0, planes] * e[slot, x0:x0 + CHUNK]
            new = new + m[1, planes] * e[slot, x0 + 2:x0 + 2 + CHUNK]
            new = new + m[2, planes] * y_low
            new = new + m[3, planes] * y_high
            new = new + m[4, planes] * z_low
            new = new + m[5, planes] * z_high
            e[new_slot, x0 + 1:x0 + 1 + CHUNK] = new
            ys[new_slot, 0, planes] = new[:, 0:1]
            ys[new_slot, 1, planes] = new[:, y - 1:y]

    for cycle in range(CYCLES):
        slot = cycle % 2
        finish(faces(3, slot))
        u = es[3][slot]
        middle = u[1:nx + 1]
        y_low, y_high = y_shift(middle, yrs[3][slot, 0], yrs[3][slot, 1])
        z_low, z_high = z_shift(middle)
        residual = fields[4] - diag[...] * middle
        around = (u[0:nx], u[2:nx + 2], y_low, y_high, z_low, z_high)
        for j in range(6):
            residual = residual + weights[j] * around[j]
        for g in range(3):
            x, y, z = shapes[g]
            first = ms[g][6] * mean(residual, g)
            fs[g][...] = first
            es[g][1, 1:x + 1] = first
            yss[g][1, 0] = first[:, 0:1]
            yss[g][1, 1] = first[:, y - 1:y]
            start(faces(g, 1))

        @pl.loop(1, SWEEPS)
        def _(repeat):
            old = lax.rem(repeat, 2)
            for g in range(3):
                finish(faces(g, old))
                sweep(g, old, 1 - old)
                start(faces(g, 1 - old))

        last = SWEEPS % 2
        for g in range(3):
            finish(faces(g, last))
        e = es[0][last, :, :, :nz]
        x = nx // 2
        even = 0.75 * e[1:x + 1] + 0.25 * e[0:x]
        odd = 0.75 * e[1:x + 1] + 0.25 * e[2:x + 2]
        update = jnp.stack([even, odd], 1).reshape((nx, ny, nz))
        e = es[1][last, 1:nx + 1, :, :nz]
        y_low, y_high = y_shift(e, yrs[1][last, 0, :, :, :nz], yrs[1][last, 1, :, :, :nz])
        even = (0.75 * e + 0.25 * y_low).reshape((rows // 2, nz))
        odd = (0.75 * e + 0.25 * y_high).reshape((rows // 2, nz))
        update = update + matmul(weave, jnp.concatenate([even, odd], 0)).reshape((nx, ny, nz))
        e = es[2][last, 1:nx + 1].reshape((rows, half + LANES))
        update = update + matmul(e, z_spread).reshape((nx, ny, nz))
        result = es[3][slot, 1:nx + 1, :, :nz] + blending * update
        if cycle == CYCLES - 1:
            out_ref[...] = result
            continue
        per = LANES // STEP
        plane_lane = iota((ny, LANES), 1)
        groups = us.shape[1]
        for q in range(groups):
            low = jnp.zeros((ny, LANES), jnp.float32)
            high = low
            for p in range(min(per, nx - q * per)):
                plane = result[q * per + p]
                here = (plane_lane >= STEP * p) & (plane_lane < STEP * p + REACH)
                first = plane[:, :LANES]
                low = jnp.where(here, pltpu.roll(first, STEP * p, 1) if p else first, low)
                high = jnp.where(
                    here, pltpu.roll(plane[:, nz - LANES:], (STEP * p + REACH) % LANES, 1), high)
            us[0, q] = low
            us[1, q] = high
        again = [
            (4, copy(us.at[0], ur.at[1], zsend.at[2], zrecv.at[2], 4)),
            (5, copy(us.at[1], ur.at[0], zsend.at[3], zrecv.at[3], 5)),
        ]
        start(again)
        es[3][1 - slot, 1:nx + 1, :, :nz] = result
        finish(again)
        for i in range(nx):
            q, p = i // per, i % per
            up = pltpu.roll(ur[1, q], (LANES - STEP * p) % LANES, 1) if p else ur[1, q]
            down = pltpu.roll(ur[0, q], (2 * LANES - REACH - STEP * p) % LANES, 1)
            es[3][1 - slot, i + 1, :, nz:] = jnp.where(
                plane_lane < REACH, up, jnp.where(plane_lane >= LANES - REACH, down, 0.0))
        send_guess(1 - slot)


def body(names, right_side, coefficients, first_guess):
    nx, ny, nz = right_side.shape
    wide = nz + LANES
    shapes = ((nx // 2, ny, wide), (nx, ny // 2, wide), (nx, ny, nz // 2 + LANES), (nx, ny, wide))
    f32 = jnp.float32
    vmem = lambda *shape: pltpu.VMEM(shape, f32)
    dma = pltpu.SemaphoreType.DMA
    groups = -(-nx // (LANES // STEP))
    scratch = [
        vmem(5, nx, ny, wide),
        vmem(6, nx, ny, wide),
        vmem(nx, ny, wide),
        tuple(vmem(2, x + 2, y, z) for x, y, z in shapes),
        tuple(vmem(2, 2, x, 1, z) for x, y, z in shapes),
        tuple(vmem(2, 2, x, 1, z) for x, y, z in shapes),
        tuple(vmem(7, x, y, z) for x, y, z in shapes[:3]),
        tuple(vmem(x, y, z) for x, y, z in shapes[:3]),
        vmem(2, 2, ny, wide),
        vmem(2, 2, nx, 1, wide),
        vmem(2, 2, nx, 1, wide),
        vmem(2, nx, ny, LANES),
        vmem(2, nx, ny, LANES),
        vmem(2, groups, ny, LANES),
        vmem(2, groups, ny, LANES),
        dma((4, 4, 2)), dma((4, 4, 2)), dma((4,)), dma((4,)), dma((4,)), dma((4,)),
    ]
    spec = pl.BlockSpec(memory_space=pltpu.VMEM)
    return pl.pallas_call(
        functools.partial(kernel, (nx, ny, nz), names),
        out_shape=jax.ShapeDtypeStruct(right_side.shape, f32),
        in_specs=[spec] * 3,
        out_specs=spec,
        scratch_shapes=scratch,
        compiler_params=pltpu.CompilerParams(
            collective_id=0, has_side_effects=True, vmem_limit_bytes=60 * 1024 * 1024),
    )(right_side, coefficients, first_guess)


def solution(mesh):
    names = tuple(mesh.axis_names)
    in_specs = (P(*names), P(None, *names), P(*names))
    return jax.shard_map(
        functools.partial(body, names), mesh=mesh, in_specs=in_specs, out_specs=P(*names),
        check_vma=False)
```

time: 624 us -> 85.2 us (0.14); the launches traced: 614 us -> 85 us
  starting transfers between devices: 300 us -> 0 us
  other arithmetic: 159 us -> 0 us
  local copies, waits for them, and re-layouts: 111 us -> 1.67 us
  Pallas kernels: 0 us -> 83.3 us
  waiting for transfers between devices: 39.8 us -> 0 us
    ppermute x108 -> x0, starting transfers between devices: 300 us -> none  [the longest x54 228 us: with_halo(): lax.ppermute(lax.slice_in_dim(block, block.shape[dim] - width, None, axis...]
    add x44 -> x0, other arithmetic: 85 us -> none  [the longest x42 83.9 us: deep_sweeps(): errors = trimmed(errors, 1) + trimmed(inside, cut) * step_term]
    pallas_call x0 -> x1, Pallas kernels: none -> 83.3 us  [body(): pl.pallas_call(functools.partial(kernel, (nx, ny, nz), names), out_shape=...]
    slice x69 -> x0, local copies, waits for them, and re-layouts: 47.4 us -> none  [the longest x49 28.3 us: with_halo(): lax.slice_in_dim(block, block.shape[dim] - width, None, axis=dim)]
    concatenate x38 -> x0, other arithmetic: 44.7 us -> none  [the longest x36 44.6 us: with_halo(): block = jnp.concatenate([low, block, high], axis=dim)]
    ppermute x108 -> x0, waiting for transfers between devices: 39.8 us -> none  [the longest x54 29.9 us: with_halo(): lax.ppermute(lax.slice_in_dim(block, 0, width, axis=dim), axis, backward)]
    ppermute x20 -> x0, local copies, waits for them, and re-layouts: 22.6 us -> none  [the longest x10 12.1 us: with_halo(): lax.ppermute(lax.slice_in_dim(block, block.shape[dim] - width, None, axis...]
    mul x23 -> x0, other arithmetic: 20.6 us -> none  [the longest x6 10.6 us: deep_sweeps(): errors = inside * (relaxation * widened_residual / diagonal)]
  transfers between devices with their start and end apart: 108 -> 0, of which waited for: 19 -> 0; matrix products, arithmetic and copies ran while one was open for 33% -> 0% of each run, Pallas kernels for 0% -> 0%
where the time goes in v1:
time: 85.2 us; the launch traced here: 85 us
  Pallas kernels  83.3 us (98%)
  local copies, waits for them, and re-layouts  1.67 us (2%)
    pallas_call x1, Pallas kernels, body(): pl.pallas_call(functools.partial(kernel, (nx, ny, nz), names), out_shape=...  83.3 us

profile of v1, /device:TPU:0, one launch (start us, length us, event | category | flops | bytes accessed | tf_op | source)
XLA Modules:
  0.0 85.0 jit_solution(15711256904037667554)
XLA Ops:
  0.0 83.3 %shard_map.37 = f32[16,16,256]{2,1,0:T(8,128)} custom-call(f32[16,16,256]{2,1,0:T(8,128)} %b_ref.1, f32[4,16,16,256]{3,2,1,0:T(8,128)} %k_ref.1, f32[16,16,256]{2,1,0:T(8,128)} %g_ref.1), custom_call_target="tpu_custom_call" | custom-call | tf_op jit(solution)/shard_map/pallas_call | solution.py:372
  83.3 1.7 %copy.5 = f32[16,16,256]{2,1,0:T(8,128)} copy(f32[16,16,256]{2,1,0:T(8,128)} %shard_map.37) | data formatting | bytes 524288

commit v2 on v1

--- a/solution.py
+++ b/solution.py
@@ -17,21 +17,24 @@
 relaxation = 0.8
 blending = 0.4
 MESH = pl.DeviceIdType.MESH
-HIGH = lax.Precision.HIGHEST
 
 
 def iota(shape, dim):
     return lax.broadcasted_iota(jnp.int32, shape, dim)
 
 
-def matmul(a, b):
-    return lax.dot_general(
-        a, b, (((1,), (0,)), ((), ())), precision=HIGH, preferred_element_type=jnp.float32
-    )
+def spread(a, b):
+    total = None
+    for _ in range(3):
+        part = a.astype(jnp.bfloat16)
+        a = a - part.astype(jnp.float32)
+        term = jnp.dot(part, b, preferred_element_type=jnp.float32)
+        total = term if total is None else total + term
+    return total
 
 
 def kernel(sizes, names, b_ref, k_ref, g_ref, out_ref, *scratch):
-    (fields, weights, diag, es, yss, yrs, ms, fs, kxr, kys, kyr, zs, zr, us, ur,
+    (fields, cells, tiles, es, yss, yrs, ms, fs, kxr, kys, kyr, zs, zr, us, ur,
      send, recv, ksend, krecv, zsend, zrecv) = scratch
     nx, ny, nz = sizes
     wide = nz + LANES
@@ -163,26 +166,40 @@
         r < nz, r // 2,
         jnp.where(r < nz + LANES // 2, half + (r - nz) // 2, half + LANES // 2 + (r - nz) // 2),
     )
-    z_mean = jnp.where(home == c, 0.5, 0.0).astype(jnp.float32)
+    z_mean = jnp.where(home == c, 0.5, 0.0).astype(jnp.bfloat16)
     rows = nx * ny
-    r, c = iota((rows // 2, rows), 0), iota((rows // 2, rows), 1)
-    y_mean = jnp.where(c // 2 == r, 0.5, 0.0).astype(jnp.float32)
-    r, c = iota((rows, rows), 0), iota((rows, rows), 1)
-    weave = jnp.where(r // 2 + (r % 2) * (rows // 2) == c, 1.0, 0.0).astype(jnp.float32)
     r, c = iota((half + LANES, nz), 0), iota((half + LANES, nz), 1)
     main = c // 2
     total = half + LANES
     side = jnp.where(c % 2 == 1, main + 1, jnp.where(main == 0, total - 1, main - 1))
-    z_spread = (jnp.where(r == main, 0.75, 0.0) + jnp.where(r == side, 0.25, 0.0)).astype(jnp.float32)
-
-    def mean(values, d):
-        if d == 0:
-            paired = values.reshape((values.shape[0] // 2, 2) + values.shape[1:])
-            return 0.5 * (paired[:, 0] + paired[:, 1])
-        flat = values.reshape((values.shape[0] * ny, wide))
-        if d == 1:
-            return matmul(y_mean, flat).reshape((nx, ny // 2, wide))
-        return matmul(flat, z_mean).reshape(shapes[2])
+    z_spread = (jnp.where(r == main, 0.75, 0.0) + jnp.where(r == side, 0.25, 0.0)).astype(jnp.bfloat16)
+
+    count = wide // LANES
+    even_rows, odd_rows = pl.ds(0, ny // 2, stride=2), pl.ds(1, ny // 2, stride=2)
+
+    def put_tiles(planes, values):
+        for t in range(values.shape[2] // LANES):
+            tiles[t, planes] = values[:, :, LANES * t:LANES * (t + 1)]
+
+    def get_tiles(planes, tiles_of=count):
+        return jnp.concatenate([tiles[t, planes] for t in range(tiles_of)], 2)
+
+    def y_mean(planes):
+        return jnp.concatenate(
+            [0.5 * (tiles[t, planes, even_rows] + tiles[t, planes, odd_rows]) for t in range(count)], 2)
+
+    def chunks(x, step=CHUNK):
+        return [slice(x0, x0 + step) for x0 in range(0, x, step)]
+
+    def below_of(ref, planes, halo):
+        if planes.start > 0:
+            return ref[planes.start - 1:planes.stop - 1]
+        return jnp.concatenate([halo, ref[0:planes.stop - 1]], 0)
+
+    def above_of(ref, planes, halo):
+        if planes.stop < ref.shape[0]:
+            return ref[planes.start + 1:planes.stop + 1]
+        return jnp.concatenate([ref[planes.start + 1:planes.stop], halo], 0)
 
     def y_shift(values, halo_low, halo_high):
         y = values.shape[1]
@@ -194,56 +211,73 @@
     def z_shift(values):
         return pltpu.roll(values, 1, 2), pltpu.roll(values, values.shape[2] - 1, 2)
 
-    def face_weights(k0, k1, k2, s, x_low, x_high, y_low, y_high):
-        pairs = [
-            (jnp.concatenate([x_low, k0[:-1]], 0), jnp.concatenate([k0[1:], x_high], 0)),
-            y_shift(k1, y_low, y_high),
-            z_shift(k2),
-        ]
+    def face_weights(k, planes, near_x, near_y):
+        k0, k1, k2 = k.at[0], k.at[1], k.at[2]
+        m1, m2 = k1[planes], k2[planes]
+        groups = (
+            (k0[planes], (below_of(k0, planes, near_x[0]), above_of(k0, planes, near_x[1]))),
+            (m1, y_shift(m1, near_y[0](planes), near_y[1](planes))),
+            (m2, z_shift(m2)),
+        )
         found = []
-        total = s
-        for k, pair in zip((k0, k1, k2), pairs):
+        total = k[3, planes]
+        for middle, pair in groups:
             for other in pair:
-                w = 0.5 * (k + other)
-                found.append(w)
-                total = total + w
+                found.append(0.5 * (middle + other))
+                total = total + found[-1]
         return found, total
 
+    for j in range(4):
+        for d in range(2):
+            factor = 0.25 if j == d else 1.0
+            if d == 0:
+                for i in range(nx // 2):
+                    cells[0][j, i] = (0.5 * factor) * (fields[j, 2 * i] + fields[j, 2 * i + 1])
+            else:
+                for planes in chunks(nx):
+                    put_tiles(planes, fields[j, planes])
+                for planes in chunks(nx):
+                    cells[1][j, planes] = y_mean(planes) * factor
     finish(edges)
-    near_x = (kxr[0, 1:2], kxr[1, 0:1])
-    near_y = (kyr[0, 1], kyr[1, 0])
-    w, total_fine = face_weights(
-        fields[0], fields[1], fields[2], fields[3], *near_x, *near_y)
-    for j in range(6):
-        weights[j] = w[j]
-    diag[...] = total_fine
+    near_rows = [kxr[0, 1], kxr[1, 0]] + [kyr[0, 1].reshape((nx, wide)), kyr[1, 0].reshape((nx, wide))]
+    flat = jnp.concatenate([fields[j].reshape((rows, wide)) for j in range(4)] + near_rows, 0)
+    flat = spread(flat, z_mean)
+    for j in range(4):
+        part = flat[rows * j:rows * (j + 1)] * (0.25 if j == 2 else 1.0)
+        cells[2][j] = part.reshape(shapes[2])
+    edge = flat[4 * rows:]
+    edge_x = [edge[0:ny][None], edge[ny:2 * ny][None]]
+    edge_y = [edge[2 * ny + nx * side:2 * ny + nx * (side + 1)].reshape((nx, 1, half + LANES)) for side in range(2)]
+    put_tiles(slice(0, 2), jnp.stack([kxr[0, 1], kxr[1, 0]]))
+    pair = y_mean(slice(0, 2))
+
+    near_xs = (
+        [0.125 * (kxr[side, 0:1] + kxr[side, 1:2]) for side in range(2)],
+        [pair[0:1], pair[1:2]],
+        edge_x,
+    )
+
+    def y_face(d, side):
+        nearest = kyr.at[side, 1 - side]
+        if d == 0:
+            return lambda planes: jnp.concatenate(
+                [0.5 * (nearest[2 * i:2 * i + 1] + nearest[2 * i + 1:2 * i + 2])
+                 for i in range(planes.start, planes.stop)], 0)
+        if d == 1:
+            return lambda planes: 0.125 * (kyr[side, 0, planes] + kyr[side, 1, planes])
+        if d == 2:
+            return lambda planes: edge_y[side][planes]
+        return lambda planes: nearest[planes]
 
     for d in range(3):
-        coarse = [mean(fields[j], d) for j in range(4)]
-        coarse[d] = coarse[d] * 0.25
-        if d == 0:
-            x_faces = [0.125 * (kxr[side, 0:1] + kxr[side, 1:2]) for side in range(2)]
-            y_faces = [
-                0.5 * (v[:, 0] + v[:, 1])
-                for v in [h.reshape((nx // 2, 2, 1, wide)) for h in near_y]
-            ]
-        elif d == 1:
-            x_faces = [
-                matmul(y_mean[: ny // 2, :ny], v[0])[None] for v in near_x
-            ]
-            y_faces = [0.125 * (kyr[side, 0] + kyr[side, 1]) for side in range(2)]
-        else:
-            x_faces = [matmul(v[0], z_mean)[None] for v in near_x]
-            y_faces = [
-                jnp.stack([matmul(jnp.broadcast_to(v[i], (8, wide)), z_mean)[0:1] for i in range(nx)])
-                for v in near_y
-            ]
-        w, total_coarse = face_weights(*coarse, *x_faces, *y_faces)
-        inside = coarse[3] > 0.0
-        scale = jnp.where(inside, relaxation / jnp.where(inside, total_coarse, 1.0), 0.0)
-        ms[d][6] = scale
-        for j in range(6):
-            ms[d][j] = w[j] * scale
+        for planes in chunks(shapes[d][0]):
+            w, total_coarse = face_weights(
+                cells[d], planes, near_xs[d], (y_face(d, 0), y_face(d, 1)))
+            inside = cells[d][3, planes] > 0.0
+            scale = jnp.where(inside, relaxation / jnp.where(inside, total_coarse, 1.0), 0.0)
+            ms[d][6, planes] = scale
+            for j in range(6):
+                ms[d][j, planes] = w[j] * scale
 
     def sweep(g, slot, new_slot):
         e, yr, ys, m, f = es[g], yrs[g], yss[g], ms[g], fs[g]
@@ -267,21 +301,37 @@
     for cycle in range(CYCLES):
         slot = cycle % 2
         finish(faces(3, slot))
-        u = es[3][slot]
-        middle = u[1:nx + 1]
-        y_low, y_high = y_shift(middle, yrs[3][slot, 0], yrs[3][slot, 1])
-        z_low, z_high = z_shift(middle)
-        residual = fields[4] - diag[...] * middle
-        around = (u[0:nx], u[2:nx + 2], y_low, y_high, z_low, z_high)
-        for j in range(6):
-            residual = residual + weights[j] * around[j]
+        u = es[3]
+        for planes in chunks(nx):
+            x0, x1 = planes.start, planes.stop
+            middle = u[slot, x0 + 1:x1 + 1]
+            y_low, y_high = y_shift(middle, yrs[3][slot, 0, planes], yrs[3][slot, 1, planes])
+            z_low, z_high = z_shift(middle)
+            w, total_fine = face_weights(
+                fields, planes, (kxr[0, 1:2], kxr[1, 0:1]), (y_face(3, 0), y_face(3, 1)))
+            residual = fields[4, planes] - total_fine * middle
+            around = (u[slot, x0:x1], u[slot, x0 + 2:x1 + 2], y_low, y_high, z_low, z_high)
+            for j in range(6):
+                residual = residual + w[j] * around[j]
+            put_tiles(planes, residual)
         for g in range(3):
             x, y, z = shapes[g]
-            first = ms[g][6] * mean(residual, g)
-            fs[g][...] = first
-            es[g][1, 1:x + 1] = first
-            yss[g][1, 0] = first[:, 0:1]
-            yss[g][1, 1] = first[:, y - 1:y]
+            if g == 2:
+                flat = get_tiles(slice(0, nx)).reshape((rows, wide))
+                whole = spread(flat, z_mean).reshape(shapes[2])
+            for planes in chunks(x):
+                if g == 0:
+                    pairs = [get_tiles(slice(2 * i, 2 * i + 2)) for i in range(planes.start, planes.stop)]
+                    first = jnp.concatenate([0.5 * (p[0:1] + p[1:2]) for p in pairs], 0)
+                elif g == 1:
+                    first = y_mean(planes)
+                else:
+                    first = whole[planes]
+                first = ms[g][6, planes] * first
+                fs[g][planes] = first
+                es[g][1, planes.start + 1:planes.stop + 1] = first
+                yss[g][1, 0, planes] = first[:, 0:1]
+                yss[g][1, 1, planes] = first[:, y - 1:y]
             start(faces(g, 1))
 
         @pl.loop(1, SWEEPS)
@@ -295,22 +345,31 @@
         last = SWEEPS % 2
         for g in range(3):
             finish(faces(g, last))
-        e = es[0][last, :, :, :nz]
-        x = nx // 2
-        even = 0.75 * e[1:x + 1] + 0.25 * e[0:x]
-        odd = 0.75 * e[1:x + 1] + 0.25 * e[2:x + 2]
-        update = jnp.stack([even, odd], 1).reshape((nx, ny, nz))
-        e = es[1][last, 1:nx + 1, :, :nz]
-        y_low, y_high = y_shift(e, yrs[1][last, 0, :, :, :nz], yrs[1][last, 1, :, :, :nz])
-        even = (0.75 * e + 0.25 * y_low).reshape((rows // 2, nz))
-        odd = (0.75 * e + 0.25 * y_high).reshape((rows // 2, nz))
-        update = update + matmul(weave, jnp.concatenate([even, odd], 0)).reshape((nx, ny, nz))
         e = es[2][last, 1:nx + 1].reshape((rows, half + LANES))
-        update = update + matmul(e, z_spread).reshape((nx, ny, nz))
-        result = es[3][slot, 1:nx + 1, :, :nz] + blending * update
+        from_z = spread(e, z_spread).reshape((nx, ny, nz))
+        for planes in chunks(nx):
+            e = es[1][last, planes.start + 1:planes.stop + 1, :, :nz]
+            y_low, y_high = y_shift(
+                e, yrs[1][last, 0, planes, :, :nz], yrs[1][last, 1, planes, :, :nz])
+            even = 0.75 * e + 0.25 * y_low
+            odd = 0.75 * e + 0.25 * y_high
+            for t in range(nz // LANES):
+                tiles[t, planes, even_rows] = even[:, :, LANES * t:LANES * (t + 1)]
+                tiles[t, planes, odd_rows] = odd[:, :, LANES * t:LANES * (t + 1)]
+        for i in range(nx // 2):
+            planes = slice(2 * i, 2 * i + 2)
+            e = es[0][last, i:i + 3, :, :nz]
+            even = 0.75 * e[1:2] + 0.25 * e[0:1]
+            odd = 0.75 * e[1:2] + 0.25 * e[2:3]
+            update = (jnp.concatenate([even, odd], 0) + get_tiles(planes, nz // LANES)) + from_z[planes]
+            final = es[3][slot, 2 * i + 1:2 * i + 3, :, :nz] + blending * update
+            if cycle == CYCLES - 1:
+                out_ref[planes] = final
+            else:
+                es[3][1 - slot, 2 * i + 1:2 * i + 3, :, :nz] = final
         if cycle == CYCLES - 1:
-            out_ref[...] = result
             continue
+        result = es[3].at[1 - slot, 1:nx + 1]
         per = LANES // STEP
         plane_lane = iota((ny, LANES), 1)
         groups = us.shape[1]
@@ -318,12 +377,11 @@
             low = jnp.zeros((ny, LANES), jnp.float32)
             high = low
             for p in range(min(per, nx - q * per)):
-                plane = result[q * per + p]
                 here = (plane_lane >= STEP * p) & (plane_lane < STEP * p + REACH)
-                first = plane[:, :LANES]
+                first = result[q * per + p, :, :LANES]
                 low = jnp.where(here, pltpu.roll(first, STEP * p, 1) if p else first, low)
                 high = jnp.where(
-                    here, pltpu.roll(plane[:, nz - LANES:], (STEP * p + REACH) % LANES, 1), high)
+                    here, pltpu.roll(result[q * per + p, :, nz - LANES:nz], (STEP * p + REACH) % LANES, 1), high)
             us[0, q] = low
             us[1, q] = high
         again = [
@@ -331,7 +389,6 @@
             (5, copy(us.at[1], ur.at[0], zsend.at[3], zrecv.at[3], 5)),
         ]
         start(again)
-        es[3][1 - slot, 1:nx + 1, :, :nz] = result
         finish(again)
         for i in range(nx):
             q, p = i // per, i % per
@@ -352,8 +409,8 @@
     groups = -(-nx // (LANES // STEP))
     scratch = [
         vmem(5, nx, ny, wide),
-        vmem(6, nx, ny, wide),
-        vmem(nx, ny, wide),
+        tuple(vmem(4, x, y, z) for x, y, z in shapes[:3]),
+        vmem(wide // LANES, nx, ny, LANES),
         tuple(vmem(2, x + 2, y, z) for x, y, z in shapes),
         tuple(vmem(2, 2, x, 1, z) for x, y, z in shapes),
         tuple(vmem(2, 2, x, 1, z) for x, y, z in shapes),

time: 85.2 us -> 78.6 us (0.923)
  Pallas kernels: 83.3 us -> 76.7 us
    pallas_call x1, Pallas kernels: 83.3 us -> 76.7 us  [body(): pl.pallas_call(functools.partial(kernel, (nx, ny, nz), names), out_shape=...]
where the time goes in v2:
time: 78.6 us; the launch traced here: 78.4 us
  Pallas kernels  76.7 us (98%)
  local copies, waits for them, and re-layouts  1.67 us (2%)
    pallas_call x1, Pallas kernels, body(): pl.pallas_call(functools.partial(kernel, (nx, ny, nz), names), out_shape=...  76.7 us
    unnamed x1, local copies, waits for them, and re-layouts  1.67 us

profile of v2, /device:TPU:0, one launch (start us, length us, event | category | flops | bytes accessed | tf_op | source)
XLA Modules:
  0.0 78.4 jit_solution(206390163195541826)
XLA Ops:
  0.0 76.7 %shard_map.37 = f32[16,16,256]{2,1,0:T(8,128)} custom-call(f32[16,16,256]{2,1,0:T(8,128)} %b_ref.1, f32[4,16,16,256]{3,2,1,0:T(8,128)} %k_ref.1, f32[16,16,256]{2,1,0:T(8,128)} %g_ref.1), custom_call_target="tpu_custom_call" | custom-call | tf_op jit(solution)/shard_map/pallas_call | solution.py:429
  76.8 1.7 %copy.5 = f32[16,16,256]{2,1,0:T(8,128)} copy(f32[16,16,256]{2,1,0:T(8,128)} %shard_map.37) | data formatting | bytes 524288

commit v3 on v2

--- a/solution.py
+++ b/solution.py
@@ -74,14 +74,17 @@
             def _():
                 c.wait_send()
 
-    def faces(g, slot):
+    def faces(g, slot, keep=(0, 1, 2, 3)):
         x = shapes[g][0]
         e, ys, yr = es[g], yss[g], yrs[g]
+        ends = (
+            (e.at[slot, 1], e.at[slot, x + 1]),
+            (e.at[slot, x], e.at[slot, 0]),
+            (ys.at[slot, 0], yr.at[slot, 1]),
+            (ys.at[slot, 1], yr.at[slot, 0]),
+        )
         return [
-            (0, copy(e.at[slot, 1], e.at[slot, x + 1], send.at[g, 0, slot], recv.at[g, 0, slot], 0)),
-            (1, copy(e.at[slot, x], e.at[slot, 0], send.at[g, 1, slot], recv.at[g, 1, slot], 1)),
-            (2, copy(ys.at[slot, 0], yr.at[slot, 1], send.at[g, 2, slot], recv.at[g, 2, slot], 2)),
-            (3, copy(ys.at[slot, 1], yr.at[slot, 0], send.at[g, 3, slot], recv.at[g, 3, slot], 3)),
+            (way, copy(*ends[way], send.at[g, way, slot], recv.at[g, way, slot], way)) for way in keep
         ]
 
     for g in range(4):
@@ -279,10 +282,12 @@
             for j in range(6):
                 ms[d][j, planes] = w[j] * scale
 
-    def sweep(g, slot, new_slot):
+    def sweep(g, slot, new_slot, keep=(0, 1, 2, 3)):
         e, yr, ys, m, f = es[g], yrs[g], yss[g], ms[g], fs[g]
         x, y, z = shapes[g]
-        for x0 in range(0, x, CHUNK):
+        order = list(range(0, x, CHUNK))
+        order = order[:1] + order[-1:] + order[1:-1]
+        for x0 in order:
             planes = slice(x0, x0 + CHUNK)
             middle = e[slot, x0 + 1:x0 + 1 + CHUNK]
             y_low, y_high = y_shift(middle, yr[slot, 0, planes], yr[slot, 1, planes])
@@ -297,6 +302,10 @@
             e[new_slot, x0 + 1:x0 + 1 + CHUNK] = new
             ys[new_slot, 0, planes] = new[:, 0:1]
             ys[new_slot, 1, planes] = new[:, y - 1:y]
+            if x0 == order[1] and 0 in keep:
+                start(faces(g, new_slot, (0, 1)))
+        if 2 in keep:
+            start(faces(g, new_slot, (2, 3)))
 
     for cycle in range(CYCLES):
         slot = cycle % 2
@@ -334,19 +343,21 @@
                 yss[g][1, 1, planes] = first[:, y - 1:y]
             start(faces(g, 1))
 
-        @pl.loop(1, SWEEPS)
+        @pl.loop(1, SWEEPS - 1)
         def _(repeat):
             old = lax.rem(repeat, 2)
             for g in range(3):
                 finish(faces(g, old))
                 sweep(g, old, 1 - old)
-                start(faces(g, 1 - old))
 
         last = SWEEPS % 2
+        needed = ((0, 1), (2, 3), ())
         for g in range(3):
-            finish(faces(g, last))
+            finish(faces(g, 1 - last))
+            sweep(g, 1 - last, last, needed[g])
         e = es[2][last, 1:nx + 1].reshape((rows, half + LANES))
         from_z = spread(e, z_spread).reshape((nx, ny, nz))
+        finish(faces(1, last, needed[1]))
         for planes in chunks(nx):
             e = es[1][last, planes.start + 1:planes.stop + 1, :, :nz]
             y_low, y_high = y_shift(
@@ -356,6 +367,7 @@
             for t in range(nz // LANES):
                 tiles[t, planes, even_rows] = even[:, :, LANES * t:LANES * (t + 1)]
                 tiles[t, planes, odd_rows] = odd[:, :, LANES * t:LANES * (t + 1)]
+        finish(faces(0, last, needed[0]))
         for i in range(nx // 2):
             planes = slice(2 * i, 2 * i + 2)
             e = es[0][last, i:i + 3, :, :nz]

time: 78.6 us -> 75.5 us (0.961)
  Pallas kernels: 76.7 us -> 73.7 us
    pallas_call x1, Pallas kernels: 76.7 us -> 73.7 us  [body(): pl.pallas_call(functools.partial(kernel, (nx, ny, nz), names), out_shape=...]
where the time goes in v3:
time: 75.5 us; the launch traced here: 75.4 us
  Pallas kernels  73.7 us (98%)
  local copies, waits for them, and re-layouts  1.67 us (2%)
    pallas_call x1, Pallas kernels, body(): pl.pallas_call(functools.partial(kernel, (nx, ny, nz), names), out_shape=...  73.7 us
    unnamed x1, local copies, waits for them, and re-layouts  1.67 us

profile of v3, /device:TPU:0, one launch (start us, length us, event | category | flops | bytes accessed | tf_op | source)
XLA Modules:
  0.0 75.4 jit_solution(15264912793130536268)
XLA Ops:
  0.0 73.7 %shard_map.37 = f32[16,16,256]{2,1,0:T(8,128)} custom-call(f32[16,16,256]{2,1,0:T(8,128)} %b_ref.1, f32[4,16,16,256]{3,2,1,0:T(8,128)} %k_ref.1, f32[16,16,256]{2,1,0:T(8,128)} %g_ref.1), custom_call_target="tpu_custom_call" | custom-call | tf_op jit(solution)/shard_map/pallas_call | solution.py:441
  73.7 1.7 %copy.5 = f32[16,16,256]{2,1,0:T(8,128)} copy(f32[16,16,256]{2,1,0:T(8,128)} %shard_map.37) | data formatting | bytes 524288

commit v4 on v3

--- a/solution.py
+++ b/solution.py
@@ -12,7 +12,7 @@
 REACH = 2 * (SWEEPS + 1)
 STEP = 20
 LANES = 128
-CHUNK = 2
+CHUNK = 1
 
 relaxation = 0.8
 blending = 0.4
@@ -197,11 +197,13 @@
     def below_of(ref, planes, halo):
         if planes.start > 0:
             return ref[planes.start - 1:planes.stop - 1]
-        return jnp.concatenate([halo, ref[0:planes.stop - 1]], 0)
+        return halo if planes.stop == 1 else jnp.concatenate([halo, ref[0:planes.stop - 1]], 0)
 
     def above_of(ref, planes, halo):
         if planes.stop < ref.shape[0]:
             return ref[planes.start + 1:planes.stop + 1]
+        if planes.stop == planes.start + 1:
+            return halo
         return jnp.concatenate([ref[planes.start + 1:planes.stop], halo], 0)
 
     def y_shift(values, halo_low, halo_high):
@@ -241,14 +243,14 @@
                     put_tiles(planes, fields[j, planes])
                 for planes in chunks(nx):
                     cells[1][j, planes] = y_mean(planes) * factor
+    for j in range(4):
+        factor = 0.25 if j == 2 else 1.0
+        for planes in chunks(nx, nx // 2):
+            flat = fields[j, planes].reshape((rows // 2, wide))
+            cells[2][j, planes] = (spread(flat, z_mean) * factor).reshape((nx // 2,) + shapes[2][1:])
     finish(edges)
     near_rows = [kxr[0, 1], kxr[1, 0]] + [kyr[0, 1].reshape((nx, wide)), kyr[1, 0].reshape((nx, wide))]
-    flat = jnp.concatenate([fields[j].reshape((rows, wide)) for j in range(4)] + near_rows, 0)
-    flat = spread(flat, z_mean)
-    for j in range(4):
-        part = flat[rows * j:rows * (j + 1)] * (0.25 if j == 2 else 1.0)
-        cells[2][j] = part.reshape(shapes[2])
-    edge = flat[4 * rows:]
+    edge = spread(jnp.concatenate(near_rows, 0), z_mean)
     edge_x = [edge[0:ny][None], edge[ny:2 * ny][None]]
     edge_y = [edge[2 * ny + nx * side:2 * ny + nx * (side + 1)].reshape((nx, 1, half + LANES)) for side in range(2)]
     put_tiles(slice(0, 2), jnp.stack([kxr[0, 1], kxr[1, 0]]))

time: 75.5 us -> 73.9 us (0.979)
  Pallas kernels: 73.7 us -> 72 us
    pallas_call x1, Pallas kernels: 73.7 us -> 72 us  [body(): pl.pallas_call(functools.partial(kernel, (nx, ny, nz), names), out_shape=...]
where the time goes in v4:
time: 73.9 us; the launch traced here: 73.7 us
  Pallas kernels  72 us (97%)
  local copies, waits for them, and re-layouts  1.67 us (2%)
    pallas_call x1, Pallas kernels, body(): pl.pallas_call(functools.partial(kernel, (nx, ny, nz), names), out_shape=...  72 us
    unnamed x1, local copies, waits for them, and re-layouts  1.67 us

profile of v4, /device:TPU:0, one launch (start us, length us, event | category | flops | bytes accessed | tf_op | source)
XLA Modules:
  0.0 73.7 jit_solution(9022506723661265912)
XLA Ops:
  0.0 72.0 %shard_map.37 = f32[16,16,256]{2,1,0:T(8,128)} custom-call(f32[16,16,256]{2,1,0:T(8,128)} %b_ref.1, f32[4,16,16,256]{3,2,1,0:T(8,128)} %k_ref.1, f32[16,16,256]{2,1,0:T(8,128)} %g_ref.1), custom_call_target="tpu_custom_call" | custom-call | tf_op jit(solution)/shard_map/pallas_call | solution.py:443
  72.0 1.7 %copy.5 = f32[16,16,256]{2,1,0:T(8,128)} copy(f32[16,16,256]{2,1,0:T(8,128)} %shard_map.37) | data formatting | bytes 524288
